TPU v7x, 128 devices: a whole 4x4x4 slice. The times are simulated.
128 devices in a mesh: expert: 32 (over z, x, core), dp: 4 (over y).
Axes of the slice: x: 4, y: 4, z: 4, core: 2. Of those that a mesh axis runs over, the one named last changes fastest.
Arguments:
- tokens: bfloat16 [16384, 2048], P(('expert', 'dp')), may hold values from -6 to 6
- out_grad: bfloat16 [16384, 2048], P(('expert', 'dp')), may hold values from -6 to 6
- route_weights: bfloat16 [16384, 8], P(('expert', 'dp')), may hold values from 0.05 to 2.5, as said below
- expert_ids: int32 [16384, 8], P(('expert', 'dp')), may hold values from 0 to 63, all different within a row; in each aligned block of 128 rows (0 to 127, 128 to 255, ...) at most 24 rows name the same one
- gate_weight: bfloat16 [64, 2048, 384], P('expert'), may hold values from -0.125 to 0.125
- up_weight: bfloat16 [64, 2048, 384], P('expert'), may hold values from -0.125 to 0.125
- down_weight: bfloat16 [64, 384, 2048], P('expert'), may hold values from -0.3125 to 0.3125
Outputs:
- grad_input: bfloat16 [16384, 2048], P(('expert', 'dp'))
- grad_gate: bfloat16 [64, 2048, 384], P('expert', 'dp')
- grad_up: bfloat16 [64, 2048, 384], P('expert', 'dp')
- grad_down: bfloat16 [64, 384, 2048], P('expert', 'dp')
- expert_load: float32 [64], replicated
Inputs may be any that keep to these rules, and one draw needn't show every extreme that they name: `expert_ids`: each row names 8 different experts. Within each aligned block of 128 rows (the rows of one device) no expert is named by more than 24 rows, a bound that some block reaches. `route_weights`: positive router weights.
All inputs are finite; a program needn't handle non-finite values.
Results may differ from a plain program's by a relative error of at most 0.009.
Values may be sent and summed in bfloat16 or wider, within the bound.
A program may use at most 192 MiB of HBM per device.

v0:
```python
import functools

import jax
import jax.numpy as jnp
from jax import lax
from jax.experimental import pallas as pl
from jax.experimental.pallas import tpu as pltpu
from jax.sharding import PartitionSpec as P

MESH = pl.DeviceIdType.MESH
CAP = 24
SIDE = 4
N_EXPERT = 32
N_DP = 4


def expert_index(z, x, core):
    return ((z % SIDE) * SIDE + x % SIDE) * 2 + core


def remote(src, dst, send_sem, recv_sem, **where):
    return pltpu.make_async_remote_copy(
        src_ref=src, dst_ref=dst, send_sem=send_sem, recv_sem=recv_sem,
        device_id=where, device_id_type=MESH,
    )


def routing_tables(ids_ref, route_ref):
    shape = (N_EXPERT, 8, 128)
    row = lax.broadcasted_iota(jnp.int32, shape, 1)
    expert = lax.broadcasted_iota(jnp.int32, shape, 0) * 2 + row % 2
    count = jnp.zeros(shape, jnp.float32)
    weight = jnp.zeros(shape, jnp.float32)
    for k in range(8):
        hit = expert == ids_ref[k:k + 1, :][None]
        count = count + jnp.where(hit, 1.0, 0.0)
        weight = weight + jnp.where(hit, route_ref[k:k + 1, :][None], 0.0)
    before = lax.broadcasted_iota(jnp.int32, (128, 128), 0) < lax.broadcasted_iota(jnp.int32, (128, 128), 1)
    earlier = jnp.dot(
        count.reshape(N_EXPERT * 8, 128).astype(jnp.bfloat16),
        jnp.where(before, 1.0, 0.0).astype(jnp.bfloat16),
        preferred_element_type=jnp.float32,
    ).reshape(shape)
    slot = jnp.where(count > 0.5, earlier, -1.0)
    expert = lax.broadcasted_iota(jnp.int32, (128, 128), 0)
    weights = jnp.zeros((128, 128), jnp.float32)
    for k in range(8):
        weights = weights + jnp.where(expert == ids_ref[k:k + 1, :], route_ref[k:k + 1, :], 0.0)
    local = lax.dot_general(
        jnp.ones((8, 128), jnp.bfloat16), weights.astype(jnp.bfloat16), (((1,), (1,)), ((), ())),
        preferred_element_type=jnp.float32,
    )
    sums = jnp.broadcast_to(local[None], shape)
    return jnp.where(row < 2, slot, jnp.where(row < 4, weight, sums))


OFFSETS = (0, -1, 1, 2)
GROUPS = (
    ((0, 0), (1, 0), (-1, 0), (0, 1), (0, -1)),
    ((-1, -1), (1, -1), (-1, 1), (1, 1)),
    ((2, 0), (0, 2), (2, -1), (-1, 2)),
    ((2, 1), (1, 2), (2, 2)),
)
PLAN = ((0, 2, 2, 1), (0, 2, 2, 1), (0, 2, 2, 1), (0, 0, 0, 0))
WIDE_D, WIDE_F, WIDE_C = 2048, 2048, 1024
MOST = 48 * 5
NT = (((1,), (1,)), ((), ()))
TN = (((0,), (0,)), ((), ()))


def dot(a, b, dims=(((1,), (0,)), ((), ()))):
    return lax.dot_general(a, b, dims, preferred_element_type=jnp.float32)


def offset_slot(d):
    return OFFSETS.index(d)


def pick_rows(meta_all, chip, weighted):
    slots = lax.broadcasted_iota(jnp.int32, (CAP, 128), 0).astype(jnp.float32)
    empty = jnp.zeros((CAP, 128), jnp.float32)
    rows = []
    for e in range(2):
        for b in range(2):
            hit = slots == meta_all[2 * chip + b, e:e + 1, :]
            value = meta_all[2 * chip + b, 2 + e:3 + e, :] if weighted else 1.0
            block = jnp.where(hit, value, 0.0)
            rows.append(jnp.concatenate([block, empty] if b == 0 else [empty, block], axis=1))
    return jnp.concatenate(rows, axis=0)


def forward_kernel(
    ids_ref, route_ref, tok_hbm, grad_hbm, gate_hbm, up_hbm, down_hbm,
    x_hbm, s_hbm, gu_hbm, h_out, mine_hbm, theirs_hbm, plane_out,
    tok_all, grad_all, meta_all, meta_send, gate, up, down, xg, sg, deltas, hid, pg, stage, flipped_picks,
    msend, mrecv, send_sems, recv_sems, dense_send, dense_recv, dense_local, local_sems,
):
    me = lax.axis_index("expert")
    z, x, core = me // (2 * SIDE), (me // 2) % SIDE, me % 2
    pair = expert_index(z, x, 1 - core)

    barrier = pltpu.get_barrier_semaphore()

    def greet(i, _):
        pl.semaphore_signal(barrier, inc=1, device_id={"expert": (me + i) % N_EXPERT}, device_id_type=MESH)
        return 0

    lax.fori_loop(1, N_EXPERT, greet, 0)

    def block(all_ref, index, half=None):
        first = (index % 2) * 128
        if half is None:
            return all_ref.at[index // 2, pl.ds(pl.multiple_of(first, 128), 128)]
        return all_ref.at[index // 2, pl.ds(pl.multiple_of(first + 64 * half, 64), 64)]

    own = [
        pltpu.make_async_copy(tok_hbm, block(tok_all, me), local_sems.at[0]),
        pltpu.make_async_copy(grad_hbm, block(grad_all, me), local_sems.at[1]),
    ]
    weights = [
        pltpu.make_async_copy(hbm, vmem, local_sems.at[2 + n])
        for n, (hbm, vmem) in enumerate(((gate_hbm, gate), (up_hbm, up), (down_hbm, down)))
    ]
    for copy in own:
        copy.start()
    meta_send[...] = routing_tables(ids_ref, route_ref)
    meta_all[me] = meta_send[me]
    for copy in own:
        copy.wait()
    pl.semaphore_wait(barrier, N_EXPERT - 1)

    arrays = ((tok_all, 0), (grad_all, 1))
    started = []
    arrived = set()

    def at(order, dp_, dq, c=None):
        c = core if c is None else c
        return expert_index(z + dp_, x + dq, c) if order == 0 else expert_index(z + dq, x + dp_, c)

    def send(order, key, ref, peer):
        copy = remote(ref, ref, send_sems.at[order, key], recv_sems.at[order, key], expert=peer)
        copy.start()
        started.append(copy)

    def arrive(order, key, dst):
        remote(dst, dst, send_sems.at[order, key], recv_sems.at[order, key], expert=pair).wait_recv()


    def first_axis(order, ref):
        send(order, 0, ref, at(order, 1, 0))
        send(order, 2, ref, at(order, -1, 0))

    def second_axis(order, j, ref):
        send(order, 4 + 4 * j, ref, at(order, 0, 1))
        send(order, 6 + 4 * j, ref, at(order, 0, -1))

    def partner(order, j, i, ref):
        send(order, 20 + 4 * j + i, ref, pair)

    def mark(order, dp_, dq):
        arrived.add((order, (dp_, dq) if order == 0 else (dq, dp_)))

    def got_first(order, all_ref, side):
        j = 1 if side == 0 else 2
        index = at(order, OFFSETS[j], 0)
        ref = block(all_ref, index)
        arrive(order, 2 * side, ref)
        send(order, 2 * side + 1, block(all_ref, index, side), at(order, 1 if side == 0 else -1, 0))
        second_axis(order, j, ref)
        partner(order, j, 0, ref)
        mark(order, OFFSETS[j], 0)

    def got_first_far(order, all_ref):
        index = at(order, 2, 0)
        arrive(order, 1, block(all_ref, index, 0))
        arrive(order, 3, block(all_ref, index, 1))
        second_axis(order, 3, block(all_ref, index))
        partner(order, 3, 0, block(all_ref, index))
        mark(order, 2, 0)

    def got_second(order, all_ref, j, side):
        i = 1 if side == 0 else 2
        index = at(order, OFFSETS[j], OFFSETS[i])
        ref = block(all_ref, index)
        arrive(order, 4 + 4 * j + 2 * side, ref)
        send(order, 5 + 4 * j + 2 * side, block(all_ref, index, side), at(order, 0, 1 if side == 0 else -1))
        partner(order, j, i, ref)
        mark(order, OFFSETS[j], OFFSETS[i])

    def got_second_far(order, all_ref, j):
        index = at(order, OFFSETS[j], 2)
        arrive(order, 5 + 4 * j, block(all_ref, index, 0))
        arrive(order, 7 + 4 * j, block(all_ref, index, 1))
        partner(order, j, 3, block(all_ref, index))
        mark(order, OFFSETS[j], 2)

    for all_ref, order in arrays:
        first_axis(order, block(all_ref, me))
    for all_ref, order in arrays:
        second_axis(order, 0, block(all_ref, me))
        mark(order, 0, 0)

    def send_table(i, _):
        peer = (me + i) % N_EXPERT
        remote(meta_send.at[peer], meta_all.at[me], msend.at[i], mrecv.at[i], expert=peer).start()
        return 0

    lax.fori_loop(1, N_EXPERT, send_table, 0)
    for all_ref, order in arrays:
        partner(order, 0, 0, block(all_ref, me))
    for copy in weights:
        copy.start()

    events = []
    for side in (0, 1):
        for all_ref, order in arrays:
            events.append(functools.partial(got_first, order, all_ref, side))
    for side in (0, 1):
        for all_ref, order in arrays:
            events.append(functools.partial(got_second, order, all_ref, 0, side))
    for all_ref, order in arrays:
        events.append(functools.partial(got_first_far, order, all_ref))
    for j in (1, 2):
        for side in (0, 1):
            for all_ref, order in arrays:
                events.append(functools.partial(got_second, order, all_ref, j, side))
    for all_ref, order in arrays:
        events.append(functools.partial(got_second_far, order, all_ref, 0))
    for side in (0, 1):
        for all_ref, order in arrays:
            events.append(functools.partial(got_second, order, all_ref, 3, side))
    for j in (1, 2, 3):
        for all_ref, order in arrays:
            events.append(functools.partial(got_second_far, order, all_ref, j))

    def run_events(count):
        for _ in range(min(count, len(events))):
            events.pop(0)()

    def dispatch(unit, k, dz, dx):
        while not ((0, (dz, dx)) in arrived and (1, (dz, dx)) in arrived):
            events.pop(0)()
        index = expert_index(z + dz, x + dx, 1 - core)
        for all_ref, order in arrays:
            j, i = (offset_slot(dz), offset_slot(dx)) if order == 0 else (offset_slot(dx), offset_slot(dz))
            arrive(order, 20 + 4 * j + i, block(all_ref, index))
        chip = index // 2
        for all_ref, target, weighted in ((tok_all, xg, False), (grad_all, sg, True)):
            pick = pick_rows(meta_all, chip, weighted)
            if not weighted:
                flat = jnp.concatenate([pick, jnp.zeros((32, 256), jnp.float32)], axis=0)
                flipped_picks[unit] = flat.T.astype(jnp.bfloat16)
            pick = pick.astype(jnp.bfloat16)

            def columns(n, _, pick=pick, all_ref=all_ref, target=target):
                cols = pl.ds(pl.multiple_of(n * WIDE_D, WIDE_D), WIDE_D)
                rows = dot(pick, all_ref[chip, :, cols]).astype(jnp.bfloat16)
                for e in range(2):
                    target[e, 48 * k:48 * k + 48, cols] = rows[48 * e:48 * e + 48]
                return 0

            lax.fori_loop(0, 2048 // WIDE_D, columns, 0)

    def forward(first, count):
        place = slice(first, first + count)

        def one(e, _):
            rows = xg[e, 0:count]
            gate_linear = dot(rows, gate[e])
            up_linear = dot(rows, up[e])
            delta_hidden = dot(sg[e, 0:count], down[e], NT)
            logistic = jax.nn.sigmoid(gate_linear)
            activated = gate_linear * logistic
            hid[e, place] = (activated * up_linear).astype(jnp.bfloat16)
            delta_gate = (delta_hidden * up_linear * logistic * (1.0 + gate_linear * (1.0 - logistic))).astype(jnp.bfloat16)
            delta_up = (delta_hidden * activated).astype(jnp.bfloat16)
            deltas[e, place, 0:384] = delta_gate
            deltas[e, place, 384:768] = delta_up

            def columns(n, _):
                at_n = pl.ds(pl.multiple_of(n * WIDE_F, WIDE_F), WIDE_F)
                pg[e, 0:count, at_n] = dot(delta_gate, gate[e, at_n, :], NT) + dot(delta_up, up[e, at_n, :], NT)
                return 0

            lax.fori_loop(0, 2048 // WIDE_F, columns, 0)
            return 0

        return one

    dense = []

    def combine(k, dz, dx):
        chip = expert_index(z + dz, x + dx, 0) // 2
        n_dense = len(dense)
        if n_dense >= 2:
            for copy in dense[n_dense - 2]:
                copy()
        here = n_dense % 2
        empty = jnp.zeros((32, WIDE_C), jnp.float32)

        def columns(n, _):
            cols = pl.ds(pl.multiple_of(n * WIDE_C, WIDE_C), WIDE_C)
            rows = jnp.concatenate([pg[0, 48 * k:48 * k + 48, cols], pg[1, 48 * k:48 * k + 48, cols], empty], axis=0)
            stage[here, :, cols] = dot(flipped_picks[n_dense], rows.astype(jnp.bfloat16)).astype(jnp.bfloat16)
            return 0

        lax.fori_loop(0, 2048 // WIDE_C, columns, 0)
        kept = pltpu.make_async_copy(
            stage.at[here, pl.ds(pl.multiple_of(core * 128, 128), 128)], mine_hbm.at[chip], dense_local.at[n_dense])
        given = remote(
            stage.at[here, pl.ds(pl.multiple_of((1 - core) * 128, 128), 128)], theirs_hbm.at[chip],
            dense_send.at[n_dense], dense_recv.at[n_dense], expert=pair)
        kept.start()
        given.start()
        dense.append((kept.wait, given.wait_send))

    tables_here = []

    def tables():
        def got_table(i, _):
            peer = (me + N_EXPERT - i) % N_EXPERT
            remote(meta_send.at[peer], meta_all.at[peer], msend.at[i], mrecv.at[i], expert=peer).wait_recv()
            return 0

        lax.fori_loop(1, N_EXPERT, got_table, 0)

    stores, kept_deltas = [], []
    run_events(4)
    tables()
    first = 0
    for g, chips in enumerate(GROUPS):
        count = 48 * len(chips)
        after_dispatch, after_one, after_two, after_combine = PLAN[g]
        for copy in stores:
            copy.wait()
        for k, (dz, dx) in enumerate(chips):
            dispatch(first // 48 + k, k, dz, dx)
            run_events(after_dispatch)
        stores = [
            pltpu.make_async_copy(xg.at[:, pl.ds(0, count)], x_hbm.at[:, pl.ds(first, count)], local_sems.at[5]),
            pltpu.make_async_copy(sg.at[:, pl.ds(0, count)], s_hbm.at[:, pl.ds(first, count)], local_sems.at[6]),
        ]
        for copy in stores:
            copy.start()
        if g == 0:
            for copy in weights:
                copy.wait()
        one = forward(first, count)
        if g < 3:
            one(0, 0)
            run_events(after_one)
            one(1, 0)
            run_events(after_two)
        else:
            lax.fori_loop(0, 2, one, 0)
        keep = pltpu.make_async_copy(
            deltas.at[:, pl.ds(first, count)], gu_hbm.at[:, pl.ds(first, count)], local_sems.at[7 + g])
        keep.start()
        kept_deltas.append(keep)
        for k, (dz, dx) in enumerate(chips):
            combine(k, dz, dx)
            run_events(after_combine)
        first += count
        if g >= 2:
            begin, end = ((0, 512), (512, 768))[g - 2]
            for e in range(2):
                h_out[e, :, begin:end] = hid[e, begin:end].astype(jnp.float32).T.astype(jnp.bfloat16)
    assert not events
    total = jnp.zeros((8, 128), jnp.float32)
    for s in range(N_EXPERT):
        total = total + meta_all[s]
    plane_out[...] = total

    def sent_table(i, _):
        peer = (me + i) % N_EXPERT
        remote(meta_send.at[peer], meta_all.at[me], msend.at[i], mrecv.at[i], expert=peer).wait_send()
        return 0

    lax.fori_loop(1, N_EXPERT, sent_table, 0)
    for copy in stores + kept_deltas:
        copy.wait()
    for copy in started:
        copy.wait_send()
    for waits in dense[-2:]:
        for wait in waits:
            wait()
    n_dense = 0
    for chips in GROUPS:
        for dz, dx in chips:
            chip = expert_index(z + dz, x + dx, 0) // 2
            remote(
                theirs_hbm.at[chip], theirs_hbm.at[chip], dense_send.at[n_dense], dense_recv.at[n_dense], expert=pair
            ).wait_recv()
            n_dense += 1


VMEM_LIMIT = 67_000_000
LOAD_SCALE = 2 * N_EXPERT / (N_EXPERT * N_DP * 128 * 8)


def forward_pass(ids, routes, tokens, grads, gate, up, down):
    vmem = pl.BlockSpec(memory_space=pltpu.VMEM)
    anywhere = pl.BlockSpec(memory_space=pl.ANY)
    rows, width = tokens.shape
    hidden = gate.shape[2]
    chips = N_EXPERT // 2
    slots = chips * 2 * CAP
    bf16 = jnp.bfloat16
    dma = pltpu.SemaphoreType.DMA
    return pl.pallas_call(
        forward_kernel,
        out_shape=(
            jax.ShapeDtypeStruct((2, slots, width), bf16),
            jax.ShapeDtypeStruct((2, slots, width), bf16),
            jax.ShapeDtypeStruct((2, slots, 2 * hidden), bf16),
            jax.ShapeDtypeStruct((2, hidden, slots), bf16),
            jax.ShapeDtypeStruct((chips, rows, width), bf16),
            jax.ShapeDtypeStruct((chips, rows, width), bf16),
            jax.ShapeDtypeStruct((8, 128), jnp.float32),
        ),
        in_specs=[vmem] * 2 + [anywhere] * 5,
        out_specs=(anywhere, anywhere, anywhere, vmem, anywhere, anywhere, vmem),
        scratch_shapes=[
            pltpu.VMEM((chips, 2 * rows, width), bf16),
            pltpu.VMEM((chips, 2 * rows, width), bf16),
            pltpu.VMEM((N_EXPERT, 8, 128), jnp.float32),
            pltpu.VMEM((N_EXPERT, 8, 128), jnp.float32),
            pltpu.VMEM(gate.shape, bf16),
            pltpu.VMEM(up.shape, bf16),
            pltpu.VMEM(down.shape, bf16),
            pltpu.VMEM((2, MOST, width), bf16),
            pltpu.VMEM((2, MOST, width), bf16),
            pltpu.VMEM((2, slots, 2 * hidden), bf16),
            pltpu.VMEM((2, slots, hidden), bf16),
            pltpu.VMEM((2, MOST, width), jnp.float32),
            pltpu.VMEM((2, 2 * rows, width), bf16),
            pltpu.VMEM((chips, 2 * rows, 128), bf16),
            dma((N_EXPERT,)), dma((N_EXPERT,)),
            dma((2, 36)), dma((2, 36)),
            dma((chips,)), dma((chips,)), dma((chips,)),
            dma((11,)),
        ],
        compiler_params=pltpu.CompilerParams(collective_id=0, has_side_effects=True, vmem_limit_bytes=VMEM_LIMIT),
        name="forward_pass",
    )(ids, routes, tokens, grads, gate, up, down)


def finish_kernel(
    x_hbm, s_hbm, gu_hbm, h_hbm, mine_hbm, theirs_hbm, sums_ref,
    gi_out, gate_out, up_out, d_out, load_out,
    xv, sv, deltas, hid, sums_out, blk, theirs, tx_gu, tx_d, far_gu, far_d, rx_gu, rx_d, q_far, q_near, p_far, p_near,
    far_send, far_recv, near_send, near_recv, qf_send, qf_recv, qn_send, qn_recv,
    pf_send, pf_recv, pn_send, pn_recv, ssend, srecv, local_sems,
):
    me = lax.axis_index("expert")
    y = lax.axis_index("dp")
    z, x, core = me // (2 * SIDE), (me // 2) % SIDE, me % 2
    peers = ((y + 1) % N_DP, (y + 3) % N_DP)
    far_y = (y + 2) % N_DP

    barrier = pltpu.get_barrier_semaphore()
    neighbours = [
        expert_index(z + 1, x, core), expert_index(z - 1, x, core),
        expert_index(z, x + 1, core), expert_index(z, x - 1, core),
    ]
    for peer in neighbours:
        pl.semaphore_signal(barrier, inc=1, device_id={"expert": peer}, device_id_type=MESH)
    for peer in (*peers, far_y):
        pl.semaphore_signal(barrier, inc=1, device_id={"dp": peer}, device_id_type=MESH)
    loads = []
    for n, (hbm, vmem) in enumerate((
        (x_hbm.at[0], xv.at[0]), (gu_hbm.at[0], deltas.at[0]), (x_hbm.at[1], xv.at[1]), (gu_hbm.at[1], deltas.at[1]),
        (s_hbm, sv), (h_hbm, hid), (mine_hbm, blk), (theirs_hbm, theirs),
    )):
        load = pltpu.make_async_copy(hbm, vmem, local_sems.at[n])
        load.start()
        loads.append(load)

    started = []

    def send(copy):
        copy.start()
        started.append(copy)

    def weight_slice(slot, e, owner):
        base = pl.multiple_of(owner * 512, 512)

        def columns(n, _):
            cols = pl.ds(pl.multiple_of(base + n * 256, 256), 256)
            rows = pl.ds(pl.multiple_of(n * 256, 256), 256)
            tx_gu[slot, e, rows] = dot(xv[e, :, cols], deltas[e], TN).astype(jnp.bfloat16)
            return 0

        lax.fori_loop(0, 2, columns, 0)

    def down_slice(slot, e, owner):
        rows = hid[e, pl.ds(pl.multiple_of(owner * 96, 96), 96), :]

        def columns(n, _):
            cols = pl.ds(pl.multiple_of(n * 1024, 1024), 1024)
            tx_d[slot, e, :, cols] = dot(rows, sv[e, :, cols]).astype(jnp.bfloat16)
            return 0

        lax.fori_loop(0, 2, columns, 0)

    def by_rows(first, count, body):
        def step(i, _):
            body(pl.ds(pl.multiple_of(first + i * 32, 32), 32))
            return 0

        lax.fori_loop(0, count // 32, step, 0)

    def wide(value):
        return value.astype(jnp.float32)

    kinds = ((weight_slice, tx_gu, far_gu, rx_gu), (down_slice, tx_d, far_d, rx_d))

    def at(order, dp_, dq):
        return (expert_index(z + dp_, x + dq, core) if order == 0 else expert_index(z + dq, x + dp_, core)) // 2

    def device(order, dp_, dq):
        return expert_index(z + dp_, x + dq, core) if order == 0 else expert_index(z + dq, x + dp_, core)

    def cols_of(h):
        return pl.ds(1024 * h, 1024)

    top, bottom = pl.ds(0, 64), pl.ds(64, 64)
    parts = (top, bottom)
    whole = pl.ds(0, 128)
    steps = (1, -1)

    for kind, (compute, tx, far, rx) in enumerate(kinds):
        for side in (0, 1):
            for load in loads[2 * side:2 * side + 2] if kind == 0 else loads[4:6] if side == 0 else ():
                load.wait()
            compute(0, side, far_y)
            if kind == 0 and side == 0:
                pl.semaphore_wait(barrier, 7)
            send(remote(tx.at[0, side], far.at[side], far_send.at[side, kind], far_recv.at[side, kind], dp=peers[side]))
    for n, other in enumerate((*peers, far_y)):
        send(remote(sums_ref, sums_out.at[n], ssend.at[n], srecv.at[n], dp=other))

    loads[6].wait()
    loads[7].wait()

    def add_partner(i, _):
        chip = i // 4
        rows = pl.ds(pl.multiple_of(i % 4 * 32, 32), 32)
        blk[chip, rows] = (wide(blk[chip, rows]) + wide(theirs[chip, rows])).astype(jnp.bfloat16)
        return 0

    lax.fori_loop(0, N_EXPERT * 2, add_partner, 0)
    for j in range(4):
        for h in range(2):
            for side in (0, 1):
                send(remote(
                    blk.at[at(h, OFFSETS[j], 2), parts[side], cols_of(h)], q_far.at[h, j, parts[side]],
                    qf_send.at[h, j, side], qf_recv.at[h, j, side], expert=device(h, 0, steps[side]),
                ))

    for kind, (compute, tx, far, rx) in enumerate(kinds):
        for side in (0, 1):
            compute(1 + side, 1 - side, peers[side])
            send(remote(
                tx.at[1 + side, 1 - side], rx.at[side, 1 - side],
                near_send.at[side, 1 - side, kind], near_recv.at[side, 1 - side, kind], dp=peers[side],
            ))

    for j in (3, 1, 2, 0):
        for h in range(2):
            for side in (0, 1):
                piece = q_far.at[h, j, parts[side]]
                remote(piece, piece, qf_send.at[h, j, side], qf_recv.at[h, j, side], expert=device(h, 0, 1)).wait_recv()
                index = at(h, OFFSETS[j], steps[side])

                def add_far(rows, index=index, h=h, j=j):
                    blk[index, rows, cols_of(h)] = (
                        wide(blk[index, rows, cols_of(h)]) + wide(q_far[h, j, rows])).astype(jnp.bfloat16)

                by_rows(64 * side, 64, add_far)
                send(remote(
                    blk.at[index, whole, cols_of(h)], q_near.at[h, j, side],
                    qn_send.at[h, j, side], qn_recv.at[h, j, side], expert=device(h, 0, steps[side]),
                ))

    for kind, (compute, tx, far, rx) in enumerate(kinds):
        for side in (0, 1):
            compute(1 + side, side, peers[side])
            piece = far.at[side]
            remote(piece, piece, far_send.at[side, kind], far_recv.at[side, kind], dp=peers[0]).wait_recv()

            def add_far(rows, tx=tx, far=far, side=side):
                tx[1 + side, side, rows] = (wide(tx[1 + side, side, rows]) + wide(far[side, rows])).astype(jnp.bfloat16)

            by_rows(0, tx.shape[2], add_far)
            send(remote(
                tx.at[1 + side, side], rx.at[side, side],
                near_send.at[side, side, kind], near_recv.at[side, side, kind], dp=peers[side],
            ))

    def second_axis_sum(h, j):
        index = at(h, OFFSETS[j], 0)
        for side in (0, 1):
            piece = q_near.at[h, j, side]
            remote(piece, piece, qn_send.at[h, j, side], qn_recv.at[h, j, side], expert=device(h, 0, 1)).wait_recv()

        def add_near(rows):
            blk[index, rows, cols_of(h)] = (
                wide(blk[index, rows, cols_of(h)]) + wide(q_near[h, j, 0, rows]) + wide(q_near[h, j, 1, rows])
            ).astype(jnp.bfloat16)

        by_rows(0, 128, add_near)
        return index

    for h in range(2):
        index = second_axis_sum(h, 3)
        for side in (0, 1):
            send(remote(
                blk.at[index, parts[side], cols_of(h)], p_far.at[h, parts[side]],
                pf_send.at[h, side], pf_recv.at[h, side], expert=device(h, steps[side], 0),
            ))
    for side in (0, 1):
        for h in range(2):
            index = second_axis_sum(h, 2 if side == 0 else 1)
            piece = p_far.at[h, parts[side]]
            remote(piece, piece, pf_send.at[h, side], pf_recv.at[h, side], expert=device(h, 1, 0)).wait_recv()

            def add_far(rows, index=index, h=h):
                blk[index, rows, cols_of(h)] = (
                    wide(blk[index, rows, cols_of(h)]) + wide(p_far[h, rows])).astype(jnp.bfloat16)

            by_rows(64 * side, 64, add_far)
            send(remote(
                blk.at[index, whole, cols_of(h)], p_near.at[h, side],
                pn_send.at[h, side], pn_recv.at[h, side], expert=device(h, steps[side], 0),
            ))
    for kind, (compute, tx, far, rx) in enumerate(kinds):
        for e in (0, 1):
            compute(3, e, y)
    for h in range(2):
        index = second_axis_sum(h, 0)
        for side in (0, 1):
            piece = p_near.at[h, side]
            remote(piece, piece, pn_send.at[h, side], pn_recv.at[h, side], expert=device(h, 1, 0)).wait_recv()

        def add_last(rows, index=index, h=h):
            gi_out[rows, cols_of(h)] = (
                wide(blk[index, rows, cols_of(h)]) + wide(p_near[h, 0, rows]) + wide(p_near[h, 1, rows])
            ).astype(jnp.bfloat16)

        by_rows(0, 128, add_last)
    for n in range(3):
        remote(sums_ref, sums_out.at[n], ssend.at[n], srecv.at[n], dp=far_y).wait_recv()
    load_out[...] = (sums_ref[...] + sums_out[0] + sums_out[1] + sums_out[2]) * LOAD_SCALE
    factor = 1.0 / N_DP
    for kind, (compute, tx, far, rx) in enumerate(kinds):
        for e in (0, 1):
            for side in (0, 1):
                piece = rx.at[side, e]
                remote(piece, piece, near_send.at[side, e, kind], near_recv.at[side, e, kind], dp=far_y).wait_recv()

            def total(rows, kind=kind, e=e, tx=tx, rx=rx):
                value = ((wide(tx[3, e, rows]) + wide(rx[0, e, rows]) + wide(rx[1, e, rows])) * factor).astype(jnp.bfloat16)
                if kind == 0:
                    gate_out[e, rows] = value[:, 0:384]
                    up_out[e, rows] = value[:, 384:768]
                else:
                    d_out[e, rows] = value

            by_rows(0, tx.shape[2], total)
    for copy in started:
        copy.wait_send()


def finish(xs, ss, gu, h, mine, theirs, sums):
    vmem = pl.BlockSpec(memory_space=pltpu.VMEM)
    anywhere = pl.BlockSpec(memory_space=pl.ANY)
    bf16 = jnp.bfloat16
    chips, rows, width = mine.shape
    hidden, slots = h.shape[1:]
    tile = (8, 128)
    wide, deep = (width // N_DP, 2 * hidden), (hidden // N_DP, width)
    near = (2, width // N_DP, hidden)
    dma = pltpu.SemaphoreType.DMA
    buf = lambda *shape: pltpu.VMEM(shape, bf16)
    return pl.pallas_call(
        finish_kernel,
        out_shape=(
            jax.ShapeDtypeStruct((rows, width), bf16),
            jax.ShapeDtypeStruct(near, bf16),
            jax.ShapeDtypeStruct(near, bf16),
            jax.ShapeDtypeStruct((2, *deep), bf16),
            jax.ShapeDtypeStruct(tile, jnp.float32),
        ),
        in_specs=[anywhere] * 6 + [vmem],
        out_specs=(vmem,) * 5,
        scratch_shapes=[
            buf(2, slots, width), buf(2, slots, width), buf(2, slots, 2 * hidden), buf(2, hidden, slots),
            pltpu.VMEM((3, *tile), jnp.float32), buf(chips, rows, width), buf(chips, rows, width),
            buf(4, 2, *wide), buf(4, 2, *deep), buf(2, *wide), buf(2, *deep), buf(2, 2, *wide), buf(2, 2, *deep),
            buf(2, 4, rows, width // 2), buf(2, 4, 2, rows, width // 2),
            buf(2, rows, width // 2), buf(2, 2, rows, width // 2),
            dma((2, 2)), dma((2, 2)), dma((2, 2, 2)), dma((2, 2, 2)),
            dma((2, 4, 2)), dma((2, 4, 2)), dma((2, 4, 2)), dma((2, 4, 2)),
            dma((2, 2)), dma((2, 2)), dma((2, 2)), dma((2, 2)),
            dma((3,)), dma((3,)), dma((8,)),
        ],
        compiler_params=pltpu.CompilerParams(collective_id=1, has_side_effects=True, vmem_limit_bytes=VMEM_LIMIT),
        name="finish",
    )(xs, ss, gu, h, mine, theirs, sums)


def shards(tokens, out_grad, route_weights, expert_ids, gate_weight, up_weight, down_weight):
    rows, width = tokens.shape
    num_experts = 2 * N_EXPERT
    routes = route_weights.astype(jnp.float32)
    xs, ss, gu, h, mine, theirs, plane = forward_pass(
        expert_ids.T, routes.T, tokens, out_grad, gate_weight, up_weight, down_weight
    )
    grad_input, grad_gate, grad_up, grad_down, load = finish(xs, ss, gu, h, mine, theirs, plane)
    return grad_input, grad_gate, grad_up, grad_down, load[4, :num_experts]


def solution(mesh):
    return jax.shard_map(
        shards,
        mesh=mesh,
        in_specs=(
            P(("expert", "dp"), None),
            P(("expert", "dp"), None),
            P(("expert", "dp"), None),
            P(("expert", "dp"), None),
            P("expert", None, None),
            P("expert", None, None),
            P("expert", None, None),
        ),
        out_specs=(
            P(("expert", "dp"), None),
            P("expert", "dp", None),
            P("expert", "dp", None),
            P("expert", "dp", None),
            P(),
        ),
        check_vma=False,
    )
```

profile of v0, /device:TPU:1, one launch (start us, length us, event | category | flops | bytes accessed | tf_op | source)
XLA Modules:
  0.0 212.2 jit_solution(9891273844892692679)
XLA Ops:
  0.6 1.3 convert_bitcast_fusion.route_ref
  1.9 116.4 %forward_pass.1 = (bf16[2,768,2048]{2,1,0:T(8,128)(2,1)}, bf16[2,768,2048]{2,1,0:T(8,128)(2,1)}, bf16[2,768,768]{2,1,0:T(8,128)(2,1)}, bf16[2,384,768]{2,1,0:T(8...) custom-call(s32[8,128]{1,0:T(8,128)} %bitcast.5, ...), custom_call_target="tpu_custom_call" | custom-call | tf_op jit(solution)/shard_map/forward_pass/pallas_call | solution.py:410
  118.3 86.8 %finish.1 = (bf16[128,2048]{1,0:T(8,128)(2,1)}, bf16[2,512,384]{2,1,0:T(8,128)(2,1)}, bf16[2,512,384]{2,1,0:T(8,128)(2,1)}, bf16[2,96,2048]{2,1,0:T(8,128)(2,1)}, f32[8,128]{1,0:T(8,128)}) custom-call(bf16[2,768,2048]{2,1,0:T(8,128)(2,1)} %get-tuple-element.17.x_hbm, bf16[2,768,2048]{2,1,0:T(8,128)(2,1)} %get-tuple-element.18.s_hbm, ...), custom_call_target="tpu_custom_call" | custom-call | tf_op jit(solution)/shard_map/finish/pallas_call | solution.py:686
  205.1 0.0 copy-start.1
  205.2 0.0 copy-start
  205.2 1.3 slice_bitcast_fusion
  206.5 1.9 copy.16
  208.4 2.1 copy.17
  210.4 0.0 copy-done.1
  210.4 0.9 copy.18
  211.3 0.0 copy-done
  211.3 0.9 copy.19
Async XLA Ops:
  205.1 5.3 %copy-start.1 = (bf16[2,512,384]{2,1,0:T(8,128)(2,1)S(1)}, bf16[2,512,384]{2,1,0:T(8,128)(2,1)}, u32[]{:S(2)}) copy-start(bf16[2,512,384]{2,1,0:T(8,128)(2,1)} %get-tuple-element.36) | copy-start | bytes 2359300
  205.2 6.2 %copy-start = (bf16[2,96,2048]{2,1,0:T(8,128)(2,1)S(1)}, bf16[2,96,2048]{2,1,0:T(8,128)(2,1)}, u32[]{:S(2)}) copy-start(bf16[2,96,2048]{2,1,0:T(8,128)(2,1)} %get-tuple-element.37) | copy-start | bytes 2359300
where the time goes:
time: 213 us; the launch traced here: 212 us
  Pallas kernels  203 us (95%)
  local copies, waits for them, and re-layouts  7.05 us (3%)
    pallas_call x1, Pallas kernels, forward_pass(): pl.pallas_call(forward_kernel, out_shape=(jax.ShapeDtypeStruct((2, slots,...  116 us
    pallas_call x1, Pallas kernels, finish(): pl.pallas_call(finish_kernel, out_shape=(jax.ShapeDtypeStruct((rows, widt...  86.8 us
    unnamed x8, local copies, waits for them, and re-layouts  5.74 us

commit v1 on v0

--- a/solution.py
+++ b/solution.py
@@ -62,6 +62,7 @@
     ((2, 1), (1, 2), (2, 2)),
 )
 PLAN = ((0, 2, 2, 1), (0, 2, 2, 1), (0, 2, 2, 1), (0, 0, 0, 0))
+STAGES = 3
 WIDE_D, WIDE_F, WIDE_C = 2048, 2048, 1024
 MOST = 48 * 5
 NT = (((1,), (1,)), ((), ()))
@@ -289,22 +290,22 @@
 
     dense = []
 
-    def combine(k, dz, dx):
+    def combine(k, dz, dx, span):
         chip = expert_index(z + dz, x + dx, 0) // 2
         n_dense = len(dense)
-        if n_dense >= 2:
-            for copy in dense[n_dense - 2]:
+        if n_dense >= STAGES:
+            for copy in dense[n_dense - STAGES]:
                 copy()
-        here = n_dense % 2
-        empty = jnp.zeros((32, WIDE_C), jnp.float32)
+        here = n_dense % STAGES
+        empty = jnp.zeros((32, span), jnp.float32)
 
         def columns(n, _):
-            cols = pl.ds(pl.multiple_of(n * WIDE_C, WIDE_C), WIDE_C)
+            cols = pl.ds(pl.multiple_of(n * span, span), span)
             rows = jnp.concatenate([pg[0, 48 * k:48 * k + 48, cols], pg[1, 48 * k:48 * k + 48, cols], empty], axis=0)
             stage[here, :, cols] = dot(flipped_picks[n_dense], rows.astype(jnp.bfloat16)).astype(jnp.bfloat16)
             return 0
 
-        lax.fori_loop(0, 2048 // WIDE_C, columns, 0)
+        lax.fori_loop(0, 2048 // span, columns, 0)
         kept = pltpu.make_async_copy(
             stage.at[here, pl.ds(pl.multiple_of(core * 128, 128), 128)], mine_hbm.at[chip], dense_local.at[n_dense])
         given = remote(
@@ -358,7 +359,7 @@
         keep.start()
         kept_deltas.append(keep)
         for k, (dz, dx) in enumerate(chips):
-            combine(k, dz, dx)
+            combine(k, dz, dx, WIDE_C if g < 3 else 2048)
             run_events(after_combine)
         first += count
         if g >= 2:
@@ -381,7 +382,7 @@
         copy.wait()
     for copy in started:
         copy.wait_send()
-    for waits in dense[-2:]:
+    for waits in dense[-STAGES:]:
         for wait in waits:
             wait()
     n_dense = 0
@@ -433,7 +434,7 @@
             pltpu.VMEM((2, slots, 2 * hidden), bf16),
             pltpu.VMEM((2, slots, hidden), bf16),
             pltpu.VMEM((2, MOST, width), jnp.float32),
-            pltpu.VMEM((2, 2 * rows, width), bf16),
+            pltpu.VMEM((STAGES, 2 * rows, width), bf16),
             pltpu.VMEM((chips, 2 * rows, 128), bf16),
             dma((N_EXPERT,)), dma((N_EXPERT,)),
             dma((2, 36)), dma((2, 36)),

time: 213 us -> 211 us (level)
  no operation moved by 1% of the time
where the time goes in v1:
time: 211 us
  Pallas kernels  202 us (96%)
  local copies, waits for them, and re-layouts  7.05 us (3%)
    pallas_call x1, Pallas kernels, forward_pass(): pl.pallas_call(forward_kernel, out_shape=(jax.ShapeDtypeStruct((2, slots,...  115 us
    pallas_call x1, Pallas kernels, finish(): pl.pallas_call(finish_kernel, out_shape=(jax.ShapeDtypeStruct((rows, widt...  86.6 us
    unnamed x8, local copies, waits for them, and re-layouts  5.74 us

profile of v1, /device:TPU:1, one launch (start us, length us, event | category | flops | bytes accessed | tf_op | source)
XLA Modules:
  0.0 210.9 jit_solution(3250241254778627235)
XLA Ops:
  0.6 1.3 convert_bitcast_fusion.route_ref
  1.9 115.3 %forward_pass.1 = (bf16[2,768,2048]{2,1,0:T(8,128)(2,1)}, bf16[2,768,2048]{2,1,0:T(8,128)(2,1)}, bf16[2,768,768]{2,1,0:T(8,128)(2,1)}, bf16[2,384,768]{2,1,0:T(8...) custom-call(s32[8,128]{1,0:T(8,128)} %bitcast.5, ...), custom_call_target="tpu_custom_call" | custom-call | tf_op jit(solution)/shard_map/forward_pass/pallas_call | solution.py:411
  117.2 86.6 %finish.1 = (bf16[128,2048]{1,0:T(8,128)(2,1)}, bf16[2,512,384]{2,1,0:T(8,128)(2,1)}, bf16[2,512,384]{2,1,0:T(8,128)(2,1)}, bf16[2,96,2048]{2,1,0:T(8,128)(2,1)}, f32[8,128]{1,0:T(8,128)}) custom-call(bf16[2,768,2048]{2,1,0:T(8,128)(2,1)} %get-tuple-element.17.x_hbm, bf16[2,768,2048]{2,1,0:T(8,128)(2,1)} %get-tuple-element.18.s_hbm, ...), custom_call_target="tpu_custom_call" | custom-call | tf_op jit(solution)/shard_map/finish/pallas_call | solution.py:687
  203.9 0.0 copy-start.1
  203.9 0.0 copy-start
  203.9 1.3 slice_bitcast_fusion
  205.2 1.9 copy.16
  207.1 2.1 copy.17
  209.2 0.0 copy-done.1
  209.2 0.9 copy.18
  210.1 0.0 copy-done
  210.1 0.9 copy.19
Async XLA Ops:
  203.9 5.3 %copy-start.1 = (bf16[2,512,384]{2,1,0:T(8,128)(2,1)S(1)}, bf16[2,512,384]{2,1,0:T(8,128)(2,1)}, u32[]{:S(2)}) copy-start(bf16[2,512,384]{2,1,0:T(8,128)(2,1)} %get-tuple-element.36) | copy-start | bytes 2359300
  203.9 6.2 %copy-start = (bf16[2,96,2048]{2,1,0:T(8,128)(2,1)S(1)}, bf16[2,96,2048]{2,1,0:T(8,128)(2,1)}, u32[]{:S(2)}) copy-start(bf16[2,96,2048]{2,1,0:T(8,128)(2,1)} %get-tuple-element.37) | copy-start | bytes 2359300
